TPU v7x, 32 devices: a whole 2x2x4 slice. The times are simulated.
32 devices in a mesh: dp: 4 (over z), fsdp: 8 (over y, x, core).
Axes of the slice: x: 2, y: 2, z: 4, core: 2. Of those that a mesh axis runs over, the one named last changes fastest.
Arguments:
- hidden_in: bfloat16 [32768, 768], P(('dp', 'fsdp')), may hold values from -6 to 6
- lengths: int32 [32], P(('dp', 'fsdp')), may hold values from 128 to 1024, as said below
- expert_ids: int32 [32768, 1], P(('dp', 'fsdp')), may hold values from 0 to 1; in each aligned block of 1024 rows (0 to 1023, 1024 to 2047, ...) at most 768 rows name the same one
- norm1_gain: bfloat16 [768], P(('dp', 'fsdp')), may hold values from 0.25 to 1.75
- norm1_bias: bfloat16 [768], P(('dp', 'fsdp')), may hold values from -2 to 2
- qkv_weight: bfloat16 [768, 2304], P(('dp', 'fsdp')), may hold values from -0.21875 to 0.21875
- attn_out_weight: bfloat16 [768, 768], P(('dp', 'fsdp')), may hold values from -1.75 to 1.75
- norm2_gain: bfloat16 [768], P(('dp', 'fsdp')), may hold values from 0.25 to 1.75
- norm2_bias: bfloat16 [768], P(('dp', 'fsdp')), may hold values from -2 to 2
- expert_in: bfloat16 [3072, 2, 768], P(('dp', 'fsdp')), may hold values from -0.21875 to 0.21875
- expert_out: bfloat16 [3072, 2, 768], P(('dp', 'fsdp')), may hold values from -0.109375 to 0.109375
- out_grad: bfloat16 [32768, 768], P(('dp', 'fsdp')), may hold values from -6 to 6
Outputs:
- hidden_out: bfloat16 [32768, 768], P(('dp', 'fsdp'))
- input_grad: bfloat16 [32768, 768], P(('dp', 'fsdp'))
- grad_norm1_gain: float32 [768], P(('dp', 'fsdp'))
- grad_norm1_bias: float32 [768], P(('dp', 'fsdp'))
- grad_qkv: float32 [768, 2304], P(('dp', 'fsdp'))
- grad_attn_out: float32 [768, 768], P(('dp', 'fsdp'))
- grad_norm2_gain: float32 [768], P(('dp', 'fsdp'))
- grad_norm2_bias: float32 [768], P(('dp', 'fsdp'))
- grad_expert_in: float32 [3072, 2, 768], P(('dp', 'fsdp'))
- grad_expert_out: float32 [3072, 2, 768], P(('dp', 'fsdp'))
Inputs may be any that keep to these rules, and one draw needn't show every extreme that they name: `lengths`: rows of a sequence past its length are padding; in every draw one sequence has exactly 1024 valid tokens. `expert_ids`: among the rows of one device at most 768 name the same expert, and in every draw some device's expert receives exactly 768.
All inputs are finite; a program needn't handle non-finite values.
Results may differ from a plain program's by a relative error of at most 0.012.
Values may be sent and summed in bfloat16 or wider, within the bound.
A program may use at most 320 MiB of HBM per device.

v0:
```python
import jax
import jax.numpy as jnp
from jax import lax
from jax.sharding import PartitionSpec as P

HEAD_DIM = 64
CAP = 768


epsilon = 1e-05
masked_score = -1e30
gelu_coeff = 0.7978845608028654


def gelu_tanh(values):
    return (
        0.5 * values * (1.0 + jnp.tanh(gelu_coeff * (values + 0.044715 * values * values * values)))
    )


def layer_norm(inputs, gain_vec, bias_vec):
    average = jnp.mean(inputs, axis=-1, keepdims=True)
    centered = inputs - average
    variance = jnp.mean(centered * centered, axis=-1, keepdims=True)
    return centered * lax.rsqrt(variance + epsilon) * gain_vec + bias_vec


def masked_scores(queries, keys_seq, anchor, valid_len, scaling):
    scores = (
        jnp.einsum("qhd,khd->hqk", queries, keys_seq, preferred_element_type=jnp.float32) * scaling
    )
    query_pos = anchor + jnp.arange(queries.shape[0])
    key_pos = jnp.arange(keys_seq.shape[0])
    allowed = (key_pos[None, :] <= query_pos[:, None]) & (key_pos[None, :] < valid_len)
    return jnp.where(allowed[None], scores, masked_score)


def body(
    hidden_in,
    lengths,
    expert_ids,
    norm1_gain,
    norm1_bias,
    qkv_weight,
    attn_out_weight,
    norm2_gain,
    norm2_bias,
    expert_in,
    expert_out,
    out_grad,
):
    tok_count, model_width = hidden_in.shape
    seq_count = lengths.shape[0]
    length = tok_count // seq_count
    head_count = model_width // HEAD_DIM
    scaling = HEAD_DIM ** (-0.5)
    experts = expert_in.shape[1]
    capacity = CAP
    block_rows = min(512, length)
    blocks = length // block_rows
    inputs = hidden_in.astype(jnp.float32)
    fetched = (
        lax.all_gather(norm1_gain, ("dp", "fsdp"), axis=0, tiled=True),
        lax.all_gather(norm1_bias, ("dp", "fsdp"), axis=0, tiled=True),
        lax.all_gather(qkv_weight, ("dp", "fsdp"), axis=0, tiled=True),
        lax.all_gather(attn_out_weight, ("dp", "fsdp"), axis=0, tiled=True),
        lax.all_gather(norm2_gain, ("dp", "fsdp"), axis=0, tiled=True),
        lax.all_gather(norm2_bias, ("dp", "fsdp"), axis=0, tiled=True),
    )

    def project_heads(weights_set):
        normed = layer_norm(
            inputs, weights_set[0].astype(jnp.float32), weights_set[1].astype(jnp.float32)
        ).astype(jnp.bfloat16)
        joint = jnp.dot(normed, weights_set[2], preferred_element_type=jnp.float32).astype(
            jnp.bfloat16
        )
        joint = joint.reshape(seq_count, length, 3, head_count, HEAD_DIM)
        return (normed, joint[:, :, 0], joint[:, :, 1], joint[:, :, 2])

    normed, queries, keys_all, values_all = project_heads(fetched)

    def attend(number):
        seq_idx = number // blocks
        anchor = number % blocks * block_rows
        query_block = lax.dynamic_slice_in_dim(queries[seq_idx], anchor, block_rows, 0)
        scores = masked_scores(query_block, keys_all[seq_idx], anchor, lengths[seq_idx], scaling)
        row_max = jnp.max(scores, axis=-1, keepdims=True)
        exponent = jnp.exp(scores - row_max)
        totals = jnp.sum(exponent, axis=-1, keepdims=True)
        probs = (exponent / totals).astype(jnp.bfloat16)
        mixed_block = jnp.einsum(
            "hqk,khd->qhd", probs, values_all[seq_idx], preferred_element_type=jnp.float32
        )
        return (mixed_block.astype(jnp.bfloat16), (row_max + jnp.log(totals))[:, :, 0])

    mixed_heads, log_totals = lax.map(attend, jnp.arange(seq_count * blocks))
    mixed_heads = mixed_heads.reshape(tok_count, model_width)
    log_totals = log_totals.reshape(seq_count, blocks, head_count, block_rows)
    residual = inputs + jnp.dot(mixed_heads, fetched[3], preferred_element_type=jnp.float32)
    normed_two = layer_norm(
        residual, fetched[4].astype(jnp.float32), fetched[5].astype(jnp.float32)
    ).astype(jnp.bfloat16)
    chosen = expert_ids[:, 0]
    onehot = (chosen[:, None] == jnp.arange(experts, dtype=jnp.int32)[None, :]).astype(jnp.int32)
    ranking = jnp.cumsum(onehot, axis=0) - 1
    slot_of = jnp.sum(onehot * ranking, axis=1)
    placed = chosen * capacity + slot_of
    source = (
        jnp.full((experts * capacity,), tok_count, jnp.int32)
        .at[placed]
        .set(jnp.arange(tok_count, dtype=jnp.int32))
    )

    def to_slots(matrix):
        padded = jnp.concatenate([matrix, jnp.zeros((1, matrix.shape[1]), matrix.dtype)], 0)
        return padded[source].reshape(experts, capacity, matrix.shape[1])

    slot_inputs = to_slots(normed_two)
    slot_grads = to_slots(out_grad)
    piece_in = lax.all_gather(expert_in, ("dp", "fsdp"), axis=0, tiled=True)
    piece_out = lax.all_gather(expert_out, ("dp", "fsdp"), axis=0, tiled=True)
    preact = jnp.einsum("ecd,jed->ecj", slot_inputs, piece_in, preferred_element_type=jnp.float32)
    activated = gelu_tanh(preact).astype(jnp.bfloat16)
    slot_outputs = jnp.einsum(
        "ecj,jed->ecd", activated, piece_out, preferred_element_type=jnp.float32
    )
    branch = slot_outputs.reshape(experts * capacity, model_width)[placed]
    hidden_out = (residual + branch).astype(jnp.bfloat16)
    cotangent = out_grad.astype(jnp.float32)
    piece_in = lax.all_gather(expert_in, ("dp", "fsdp"), axis=0, tiled=True)
    piece_out = lax.all_gather(expert_out, ("dp", "fsdp"), axis=0, tiled=True)
    preact = jnp.einsum("ecd,jed->ecj", slot_inputs, piece_in, preferred_element_type=jnp.float32)
    activated = gelu_tanh(preact).astype(jnp.bfloat16)
    dactivated = jnp.einsum(
        "ecd,jed->ecj", slot_grads, piece_out, preferred_element_type=jnp.float32
    )
    dpreact = jax.vjp(gelu_tanh, preact)[1](dactivated)[0].astype(jnp.bfloat16)
    back_in = jnp.einsum("ecj,jed->ecd", dpreact, piece_in, preferred_element_type=jnp.float32)
    back_in, activations, slopes = (back_in, activated, dpreact)
    grad_in_part = jnp.einsum(
        "ecj,ecd->jed", slopes, slot_inputs, preferred_element_type=jnp.float32
    )
    grad_out_part = jnp.einsum(
        "ecj,ecd->jed", activations, slot_grads, preferred_element_type=jnp.float32
    )
    expert_both = lax.psum_scatter(
        jnp.stack([grad_in_part, grad_out_part], 1), ("dp", "fsdp"), scatter_dimension=0, tiled=True
    )
    again = (
        lax.all_gather(norm1_gain, ("dp", "fsdp"), axis=0, tiled=True),
        lax.all_gather(norm1_bias, ("dp", "fsdp"), axis=0, tiled=True),
        lax.all_gather(qkv_weight, ("dp", "fsdp"), axis=0, tiled=True),
        lax.all_gather(attn_out_weight, ("dp", "fsdp"), axis=0, tiled=True),
        lax.all_gather(norm2_gain, ("dp", "fsdp"), axis=0, tiled=True),
        lax.all_gather(norm2_bias, ("dp", "fsdp"), axis=0, tiled=True),
    )
    normed_back, queries_back, keys_back, values_back = project_heads(again)
    dnormed_two = back_in.reshape(experts * capacity, model_width)[placed]
    pull_two = jax.vjp(
        layer_norm, residual, again[4].astype(jnp.float32), again[5].astype(jnp.float32)
    )[1]
    dres_norm, dgain_two, dbias_two = pull_two(dnormed_two)
    dresidual = cotangent + dres_norm
    dproj = dresidual.astype(jnp.bfloat16)
    grad_proj = jnp.einsum("td,te->de", mixed_heads, dproj, preferred_element_type=jnp.float32)
    dmixed = jnp.einsum("te,de->td", dproj, again[3], preferred_element_type=jnp.float32).astype(
        jnp.bfloat16
    )
    dmixed = dmixed.reshape(seq_count, length, head_count, HEAD_DIM)

    def seq_back(seq_idx):
        keys_seq = keys_back[seq_idx]
        values_seq = values_back[seq_idx]
        valid_len = lengths[seq_idx]

        def block_back(running, block_idx):
            dkeys, dvalues = running
            anchor = block_idx * block_rows
            query_block = lax.dynamic_slice_in_dim(queries_back[seq_idx], anchor, block_rows, 0)
            grad_block = lax.dynamic_slice_in_dim(dmixed[seq_idx], anchor, block_rows, 0)
            scores = masked_scores(query_block, keys_seq, anchor, valid_len, scaling)
            probs_raw = jnp.exp(scores - log_totals[seq_idx, block_idx][:, :, None])
            dprobs = jnp.einsum(
                "qhd,khd->hqk", grad_block, values_seq, preferred_element_type=jnp.float32
            )
            delta = jnp.sum(dprobs * probs_raw, axis=-1, keepdims=True)
            dscores = (probs_raw * (dprobs - delta)).astype(jnp.bfloat16)
            dqueries = (
                jnp.einsum("hqk,khd->qhd", dscores, keys_seq, preferred_element_type=jnp.float32)
                * scaling
            )
            dkeys = (
                dkeys
                + jnp.einsum(
                    "hqk,qhd->khd", dscores, query_block, preferred_element_type=jnp.float32
                )
                * scaling
            )
            dvalues = dvalues + jnp.einsum(
                "hqk,qhd->khd",
                probs_raw.astype(jnp.bfloat16),
                grad_block,
                preferred_element_type=jnp.float32,
            )
            return ((dkeys, dvalues), dqueries)

        head_zero = jnp.zeros((length, head_count, HEAD_DIM), jnp.float32)
        (dkeys, dvalues), dqueries = lax.scan(
            block_back, (head_zero, head_zero), jnp.arange(blocks)
        )
        dqueries = dqueries.reshape(length, head_count, HEAD_DIM)
        return jnp.stack([dqueries, dkeys, dvalues], 1).astype(jnp.bfloat16)

    djoint = lax.map(seq_back, jnp.arange(seq_count)).reshape(tok_count, 3 * model_width)
    grad_joint = jnp.einsum("td,te->de", normed_back, djoint, preferred_element_type=jnp.float32)
    dnormed = jnp.einsum("te,de->td", djoint, again[2], preferred_element_type=jnp.float32)
    pull_one = jax.vjp(
        layer_norm, inputs, again[0].astype(jnp.float32), again[1].astype(jnp.float32)
    )[1]
    dinput_norm, dgain_one, dbias_one = pull_one(dnormed)
    input_grad = (dresidual + dinput_norm).astype(jnp.bfloat16)
    summed = (
        lax.psum_scatter(dgain_one, ("dp", "fsdp"), scatter_dimension=0, tiled=True),
        lax.psum_scatter(dbias_one, ("dp", "fsdp"), scatter_dimension=0, tiled=True),
        lax.psum_scatter(grad_joint, ("dp", "fsdp"), scatter_dimension=0, tiled=True),
        lax.psum_scatter(grad_proj, ("dp", "fsdp"), scatter_dimension=0, tiled=True),
        lax.psum_scatter(dgain_two, ("dp", "fsdp"), scatter_dimension=0, tiled=True),
        lax.psum_scatter(dbias_two, ("dp", "fsdp"), scatter_dimension=0, tiled=True),
    )
    return (
        hidden_out,
        input_grad,
        summed[0],
        summed[1],
        summed[2],
        summed[3],
        summed[4],
        summed[5],
        expert_both[:, 0],
        expert_both[:, 1],
    )


def solution(mesh):
    in_specs = (
        P(("dp", "fsdp"), None),
        P(("dp", "fsdp")),
        P(("dp", "fsdp"), None),
        P(("dp", "fsdp")),
        P(("dp", "fsdp")),
        P(("dp", "fsdp"), None),
        P(("dp", "fsdp"), None),
        P(("dp", "fsdp")),
        P(("dp", "fsdp")),
        P(("dp", "fsdp"), None, None),
        P(("dp", "fsdp"), None, None),
        P(("dp", "fsdp"), None),
    )
    out_specs = (
        P(("dp", "fsdp"), None),
        P(("dp", "fsdp"), None),
        P(("dp", "fsdp")),
        P(("dp", "fsdp")),
        P(("dp", "fsdp"), None),
        P(("dp", "fsdp"), None),
        P(("dp", "fsdp")),
        P(("dp", "fsdp")),
        P(("dp", "fsdp"), None, None),
        P(("dp", "fsdp"), None, None),
    )
    return jax.shard_map(body, mesh=mesh, in_specs=in_specs, out_specs=out_specs, check_vma=False)
```

profile of v0, /device:TPU:0, one launch (start us, length us, event | category | flops | bytes accessed | tf_op | source)
XLA Modules:
  0.0 1227.1 jit_solution(1265981327498537367)
XLA Ops:
  15.7 42.2 %all-reduce.12 = (bf16[768]{0:T(1024)(128)(2,1)S(1)}, bf16[768]{0:T(1024)(128)(2,1)S(1)}, bf16[768]{0:T(1024)(128)(2,1)S(1)}, bf16[768]{0:T(1024)(128)(2,1)S(1)}) all-reduce(bf16[768]{0:T(1024)(128)(2,1)S(1)} %dynamic-update-slice.1, bf16[768]{0:T(1024)(128)(2,1)S(1)} %dynamic-update-slice, ...), channel_id=1, replica_groups=mesh['dp'=4,'fsdp'=8] {'dp','fsdp'}, use_global_device_ids=true, to_apply=%add.3 | all-reduce | flops 3072 | bytes 12288
  63.2 4.5 scatter_custom_fusion
  69.3 5.7 gather_fusion.2
  75.0 8.0 convolution_convert_fusion
  83.0 6.6 copy.40
  89.6 5.2 slice_bitcast_fusion.1
  94.8 77.1 %while.39 = (s32[]{:T(128)}, bf16[2,512,12,64]{1,3,2,0:T(8,128)(2,1)}, f32[2,12,512]{2,1,0:T(8,128)S(1)}, s32[2]{0:T(128)S(1)}, s32[1]{0:T(128)}, /*index=5*/bf1...) while((s32[]{:T(128)}, ...), condition=%wide.region_5.6_spmd, body=%wide.region_2.5_spmd.sunk | while | flops 1687547392 | bytes 189495664 | solution.py:97
  98.4 10.6 fusion.122
  109.1 12.4 %fusion.123 = f32[12,512]{1,0:T(8,128)S(1)} fusion(f32[12,512,1024]{2,1,0:T(8,128)} %get-tuple-element.466, f32[12,512]{1,0:T(8,128)S(1)} %get-tuple-element.467, pred[512,1024]{1,0:T(8,128)(4,1)S(1)} %fusion.121), kind=kLoop, calls=%fused_computation.9.clone.1 | loop fusion | flops 25159680 | bytes 25739264 | tf_op jit(solution)/shard_map/while/body/eval_jaxpr/reduce_sum | solution.py:90
  124.7 8.5 fusion.124
  136.8 10.7 fusion.122
  147.5 12.3 %fusion.123 = f32[12,512]{1,0:T(8,128)S(1)} fusion(f32[12,512,1024]{2,1,0:T(8,128)} %get-tuple-element.466, f32[12,512]{1,0:T(8,128)S(1)} %get-tuple-element.467, pred[512,1024]{1,0:T(8,128)(4,1)S(1)} %fusion.121), kind=kLoop, calls=%fused_computation.9.clone.1 | loop fusion | flops 25159680 | bytes 25739264 | tf_op jit(solution)/shard_map/while/body/eval_jaxpr/reduce_sum | solution.py:90
  163.2 8.5 fusion.124
  182.8 5.6 gather_fusion
  188.5 25.6 %all-gather.11.cloned.1.call-done = bf16[3072,2,768]{2,0,1:T(8,128)(2,1)} async-done(((bf16[96,2,768]{2,0,1:T(8,128)(2,1)}), bf16[3072,2,768]{2,0,1:T(8,128)(2,1)}) %all-gather.11.cloned.1.call-update) | async-done | bytes 9437200 | tf_op jit(solution)/shard_map/all_gather | solution.py:122
  214.1 14.5 %fusion.76 = f32[2,768,3072]{2,1,0:T(8,128)} fusion(bf16[2,768,768]{2,1,0:T(8,128)(2,1)} %bitcast.184, bf16[3072,2,768]{2,0,1:T(8,128)(2,1)} %all-gather.11.cloned.1.call-done), kind=kOutput, calls=%fused_computation.136 | convolution fusion | flops 7247757312 | bytes 30670848 | tf_op jit(solution)/shard_map/ecd,jed->ecj/dot_general | solution.py:135
  228.6 69.5 %all-gather.9.cloned.1.call-done = bf16[3072,2,768]{2,0,1:T(8,128)(2,1)} async-done(((bf16[96,2,768]{2,0,1:T(8,128)(2,1)}), bf16[3072,2,768]{2,0,1:T(8,128)(2,1)}) %all-gather.9.cloned.1.call-update) | async-done | bytes 9437200 | tf_op jit(solution)/shard_map/all_gather | solution.py:121
  298.2 28.3 %fusion.47 = (bf16[2,768,3072]{2,1,0:T(8,128)(2,1)}, f32[2,768,3072]{2,1,0:T(8,128)}) fusion(f32[2,768,3072]{2,1,0:T(8,128)} %fusion.76, bf16[2,768,768]{2,1,0:T(8,128)(2,1)S(1)} %bitcast.186, bf16[3072,2,768]{2,0,1:T(8,128)(2,1)} %all-gather.9.cloned.1.call-done), kind=kOutput, calls=%fused_computation.65 | convolution fusion | flops 7361003520 | bytes 58982400 | tf_op jit(solution)/shard_map/ecd,jed->ecj/dot_general | solution.py:123
  326.5 14.6 %convolution_bitcast_fusion.1 = f32[3072,1,2,768]{0,3,2,1:T(8,128)} fusion(bf16[2,768,768]{2,1,0:T(8,128)(2,1)S(1)} %bitcast.187, bf16[2,768,3072]{2,1,0:T(8,128)(2,1)} %get-tuple-element.352), kind=kOutput, calls=%fused_computation.70 | convolution fusion | flops 7247757312 | bytes 30670848 | tf_op jit(solution)/shard_map/ecj,ecd->jed/dot_general | solution.py:141
  341.1 15.7 %convolution_bitcast_fusion = f32[3072,1,2,768]{0,3,2,1:T(8,128)} fusion(bf16[2,768,768]{2,1,0:T(8,128)(2,1)S(1)} %bitcast.185, f32[2,768,3072]{2,1,0:T(8,128)} %get-tuple-element.353), kind=kOutput, calls=%fused_computation.69 | convolution fusion | flops 7290224640 | bytes 40108032 | tf_op jit(solution)/shard_map/ecj,ecd->jed/dot_general | solution.py:144
  356.8 28.3 %pad_maximum_fusion = f32[3072,2,2,768]{0,3,2,1:T(8,128)} fusion(f32[3072,1,2,768]{0,3,2,1:T(8,128)} %convolution_bitcast_fusion, f32[3072,1,2,768]{0,3,2,1:T(8,128)} %convolution_bitcast_fusion.1), kind=kLoop, calls=%fused_computation.57 | loop fusion | flops 9437184 | bytes 75497472 | tf_op jit(solution)/shard_map/stack | solution.py:148
  385.1 55.4 %copy.47 = f32[3072,2,2,768]{3,2,1,0:T(2,128)} copy(f32[3072,2,2,768]{0,3,2,1:T(8,128)} %pad_maximum_fusion) | data formatting | bytes 75497472 | tf_op jit(solution)/shard_map/stack | solution.py:148
  441.2 15.7 %fusion.77 = f32[2,768,768]{2,1,0:T(8,128)} fusion(bf16[2,768,3072]{2,1,0:T(8,128)(2,1)} %get-tuple-element.352, bf16[3072,2,768]{2,0,1:T(8,128)(2,1)} %all-gather.9.cloned.1.call-done), kind=kOutput, calls=%fused_computation.137 | convolution fusion | flops 7247757312 | bytes 23592960 | tf_op jit(solution)/shard_map/ecj,jed->ecd/dot_general | solution.py:139
  456.8 8.3 gather_fusion.3
  465.2 16.9 %fusion.72 = f32[2,768,768]{2,1,0:T(8,128)} fusion(bf16[3072,2,768]{2,0,1:T(8,128)(2,1)} %all-gather.11.cloned.1.call-done, f32[2,768,3072]{2,1,0:T(8,128)} %get-tuple-element.353), kind=kOutput, calls=%fused_computation.132 | convolution fusion | flops 7290224640 | bytes 33030144 | tf_op jit(solution)/shard_map/ecj,jed->ecd/dot_general | solution.py:125
  482.0 8.4 gather_fusion.1
  490.5 5.0 multiply_reduce_fusion.1
  506.1 4.4 convolution_convert_fusion.1
  510.5 187.7 %while.40 = (s32[]{:T(128)}, f32[1024,12,64]{0,2,1:T(8,128)S(1)}, f32[1024,12,64]{0,2,1:T(8,128)}, bf16[2,512,12,64]{1,3,2,0:T(8,128)(2,1)}, s32[2]{0:T(128)S(1)...) while((s32[]{:T(128)}, f32[1024,12,64]{0,2,1:T(8,128)S(1)}, ...), condition=%wide.region_16.17_spmd.clone, body=%wide.region_14.16_spmd.clone.sunk | while | flops 4126273024 | bytes 221436240 | solution.py:209
  515.2 14.3 %fusion.134 = f32[12,512,1024]{2,1,0:T(8,128)} fusion(bf16[1024,12,64]{0,2,1:T(8,128)(2,1)} %get-tuple-element.559, bf16[1,1024,12,64]{1,3,2,0:T(8,128)(2,1)} %get-tuple-element.557, s32[]{:T(128)S(6)} %select_n.112), kind=kOutput, calls=%fused_computation.42.clone.1 | convolution fusion | flops 805306368 | bytes 27525124 | tf_op jit(solution)/shard_map/while/body/eval_jaxpr/while/body/eval_jaxpr/qhd,khd->hqk/dot_general | solution.py:30
  529.5 15.1 %bitcast_add_fusion.5 = f32[1024,12,64]{0,2,1:T(8,128)} fusion(f32[1024,12,64]{0,2,1:T(8,128)} %get-tuple-element.538, f32[12,512,1024]{2,1,0:T(8,128)} %fusion.134, f32[12,512]{1,0:T(8,128)S(1)} %dynamic-slice_bitcast_fusion.4, pred[512,1024]{1,0:T(8,128)(4,1)S(1)} %fusion.135, pred[]{:T(512)S(6)} %compare.8, ...), kind=kOutput, calls=%fused_computation.33.clone.1 | convolution fusion | flops 832045056 | bytes 32800772 | tf_op jit(solution)/shard_map/while/body/eval_jaxpr/while/body/eval_jaxpr/hqk,qhd->khd/dot_general | solution.py:200
  544.6 18.4 %multiply_reduce_fusion.5 = (f32[12,512]{1,0:T(8,128)S(1)}, f32[12,512,1024]{2,1,0:T(8,128)}) fusion(f32[12,512,1024]{2,1,0:T(8,128)} %fusion.134, f32[12,512]{1,0:T(8,128)S(1)} %dynamic-slice_bitcast_fusion.4, pred[512,1024]{1,0:T(8,128)(4,1)} %copy-done.1, bf16[1024,12,64]{0,2,1:T(8,128)(2,1)} %get-tuple-element.562, ...), kind=kOutput, calls=%fused_computation.28.clone.1 | convolution fusion | flops 836757504 | bytes 53264388 | tf_op jit(solution)/shard_map/while/body/eval_jaxpr/while/body/eval_jaxpr/qhd,khd->hqk/dot_general | solution.py:184
  563.1 24.3 %multiply_convert_fusion.5 = bf16[12,512,1024]{2,1,0:T(8,128)(2,1)} fusion(f32[12,512,1024]{2,1,0:T(8,128)} %get-tuple-element.479, f32[12,512,1024]{2,1,0:T(8,128)} %fusion.134, f32[12,512]{1,0:T(8,128)S(1)} %get-tuple-element.480, f32[12,512]{1,0:T(8,128)S(1)} %dynamic-slice_bitcast_fusion.4, pred[512,1024]{1,0:T(8,128)(4,1)} %copy-done.1), kind=kLoop, calls=%fused_computation.27.clone.1 | loop fusion | flops 37748736 | bytes 63488000 | tf_op jit(solution)/shard_map/while/body/eval_jaxpr/while/body/eval_jaxpr/convert_element_type | solution.py:188
  587.4 10.0 bitcast_dynamic-update-slice_fusion.5
  597.4 7.7 bitcast_add_fusion.4
  609.4 14.2 %fusion.134 = f32[12,512,1024]{2,1,0:T(8,128)} fusion(bf16[1024,12,64]{0,2,1:T(8,128)(2,1)} %get-tuple-element.559, bf16[1,1024,12,64]{1,3,2,0:T(8,128)(2,1)} %get-tuple-element.557, s32[]{:T(128)S(6)} %select_n.112), kind=kOutput, calls=%fused_computation.42.clone.1 | convolution fusion | flops 805306368 | bytes 27525124 | tf_op jit(solution)/shard_map/while/body/eval_jaxpr/while/body/eval_jaxpr/qhd,khd->hqk/dot_general | solution.py:30
  623.7 15.6 %bitcast_add_fusion.5 = f32[1024,12,64]{0,2,1:T(8,128)} fusion(f32[1024,12,64]{0,2,1:T(8,128)} %get-tuple-element.538, f32[12,512,1024]{2,1,0:T(8,128)} %fusion.134, f32[12,512]{1,0:T(8,128)S(1)} %dynamic-slice_bitcast_fusion.4, pred[512,1024]{1,0:T(8,128)(4,1)S(1)} %fusion.135, pred[]{:T(512)S(6)} %compare.8, ...), kind=kOutput, calls=%fused_computation.33.clone.1 | convolution fusion | flops 832045056 | bytes 32800772 | tf_op jit(solution)/shard_map/while/body/eval_jaxpr/while/body/eval_jaxpr/hqk,qhd->khd/dot_general | solution.py:200
  639.3 18.3 %multiply_reduce_fusion.5 = (f32[12,512]{1,0:T(8,128)S(1)}, f32[12,512,1024]{2,1,0:T(8,128)}) fusion(f32[12,512,1024]{2,1,0:T(8,128)} %fusion.134, f32[12,512]{1,0:T(8,128)S(1)} %dynamic-slice_bitcast_fusion.4, pred[512,1024]{1,0:T(8,128)(4,1)} %copy-done.1, bf16[1024,12,64]{0,2,1:T(8,128)(2,1)} %get-tuple-element.562, ...), kind=kOutput, calls=%fused_computation.28.clone.1 | convolution fusion | flops 836757504 | bytes 53264388 | tf_op jit(solution)/shard_map/while/body/eval_jaxpr/while/body/eval_jaxpr/qhd,khd->hqk/dot_general | solution.py:184
  657.5 22.9 %multiply_convert_fusion.5 = bf16[12,512,1024]{2,1,0:T(8,128)(2,1)} fusion(f32[12,512,1024]{2,1,0:T(8,128)} %get-tuple-element.479, f32[12,512,1024]{2,1,0:T(8,128)} %fusion.134, f32[12,512]{1,0:T(8,128)S(1)} %get-tuple-element.480, f32[12,512]{1,0:T(8,128)S(1)} %dynamic-slice_bitcast_fusion.4, pred[512,1024]{1,0:T(8,128)(4,1)} %copy-done.1), kind=kLoop, calls=%fused_computation.27.clone.1 | loop fusion | flops 37748736 | bytes 63488000 | tf_op jit(solution)/shard_map/while/body/eval_jaxpr/while/body/eval_jaxpr/convert_element_type | solution.py:188
  680.5 10.1 bitcast_dynamic-update-slice_fusion.5
  690.6 7.4 bitcast_add_fusion.4
  711.6 6.8 fusion.68
  718.4 7.8 fusion.73
  728.0 39.9 %all-reduce.11 = (f32[768]{0:T(1024)S(1)}, f32[768]{0:T(1024)S(1)}, f32[768]{0:T(1024)S(1)}, f32[768]{0:T(1024)S(1)}) all-reduce(f32[768]{0:T(1024)S(1)} %get-tuple-element.285, f32[768]{0:T(1024)S(1)} %get-tuple-element.288, f32[768]{0:T(1024)S(1)} %copy-done.46, ...), channel_id=2, replica_groups=mesh['dp'=4,'fsdp'=8] {'dp','fsdp'}, use_global_device_ids=true, to_apply=%region_20.21.clone | all-reduce | flops 3072 | bytes 24576
  770.2 4.5 add_convert_fusion
  774.8 215.2 %all-reduce.15.cloned.1.call-done = f32[3072,2,2,768]{3,2,1,0:T(2,128)} async-done(((f32[3072,2,2,768]{3,2,1,0:T(2,128)}), f32[3072,2,2,768]{3,2,1,0:T(2,128)}) %all-reduce.15.cloned.1.call-update) | async-done | bytes 37748752
  992.7 102.1 %reduce-scatter.5.cloned.1.call-done = f32[24,768]{1,0:T(8,128)} async-done(((f32[768,768]{1,0:T(8,128)}), f32[24,768]{1,0:T(8,128)}) %reduce-scatter.5.cloned.1.call-update) | async-done | bytes 73744 | tf_op jit(solution)/shard_map/reduce_scatter | solution.py:227
  1094.7 125.3 %reduce-scatter.3.cloned.1.call-done = f32[24,2304]{1,0:T(8,128)} async-done(((f32[768,2304]{1,0:T(8,128)}), f32[24,2304]{1,0:T(8,128)}) %reduce-scatter.3.cloned.1.call-update) | async-done | bytes 221200 | tf_op jit(solution)/shard_map/reduce_scatter | solution.py:226
  (210 shorter events, 70.4 us)
Async XLA Ops:
  7.2 53.6 %copy-start.8 = (bf16[1024,768]{1,0:T(8,128)(2,1)S(1)}, bf16[1024,768]{1,0:T(8,128)(2,1)}, u32[]{:S(2)}) copy-start(bf16[1024,768]{1,0:T(8,128)(2,1)} %param.16) | copy-start | bytes 4718596
  7.2 54.3 %copy-start.42 = (s32[1024,1]{0,1:T(1,128)S(1)}, s32[1024,1]{0,1:T(1,128)}, u32[]{:S(2)}) copy-start(s32[1024,1]{0,1:T(1,128)} %param.18) | copy-start | bytes 12292
  7.2 67.8 %all-gather.5.cloned.1.call-start = ((), (), s32[]{:S(2)}) async-start(), calls=%async_computation.2 | async-start | bytes 3649536 | tf_op jit(solution)/shard_map/all_gather | solution.py:65
  7.9 169.2 %all-gather.7.cloned.1.call-start = ((), (), s32[]{:S(2)}) async-start(), calls=%async_computation.3 | async-start | bytes 1216512 | tf_op jit(solution)/shard_map/all_gather | solution.py:66
  8.7 205.4 %all-gather.11.cloned.1.call-start = ((), (), s32[]{:S(2)}) async-start(), calls=%async_computation.5 | async-start | bytes 9732096 | tf_op jit(solution)/shard_map/all_gather | solution.py:122
  10.5 287.7 %all-gather.9.cloned.1.call-start = ((), (), s32[]{:S(2)}) async-start(), calls=%async_computation.4 | async-start | bytes 9732096 | tf_op jit(solution)/shard_map/all_gather | solution.py:121
  12.2 977.8 %all-reduce.15.cloned.1.call-start = ((), (), s32[]{:S(2)}) async-start(), calls=%async_computation.8 | async-start | bytes 75497472
  57.9 17.1 %copy-start.50 = (f32[768]{0:T(1024)}, f32[768]{0:T(1024)S(1)}, u32[]{:S(2)}) copy-start(f32[768]{0:T(1024)S(1)} %convert_element_type.88) | copy-start | bytes 9220
  57.9 17.1 %copy-start.34 = (f32[768]{0:T(1024)}, f32[768]{0:T(1024)S(1)}, u32[]{:S(2)}) copy-start(f32[768]{0:T(1024)S(1)} %convert_element_type.87) | copy-start | bytes 9220
  60.8 14.2 %copy-start.28 = (f32[1024]{0:T(1024)}, f32[1024]{0:T(1024)S(1)}, u32[]{:S(2)}) copy-start(f32[1024]{0:T(1024)S(1)} %broadcast_multiply_fusion.1) | copy-start | bytes 12292
  61.4 6.3 copy-start.38
  61.5 13.5 %copy-start.36 = (f32[1024]{0:T(1024)}, f32[1024]{0:T(1024)S(1)}, u32[]{:S(2)}) copy-start(f32[1024]{0:T(1024)S(1)} %fusion.66) | copy-start | bytes 12292
  67.7 7.2 copy-start.26
  98.4 23.0 %copy-start.19 = (bf16[1,1024,12,64]{1,3,2,0:T(8,128)(2,1)S(1)}, bf16[1,1024,12,64]{1,3,2,0:T(8,128)(2,1)}, u32[]{:S(2)}) copy-start(bf16[1,1024,12,64]{1,3,2,0:T(8,128)(2,1)} %get-tuple-element.514) | copy-start | bytes 4718596 | tf_op jit(solution)/shard_map/while
  109.1 15.6 %copy-start = (f32[12,512,1024]{2,1,0:T(8,128)S(1)}, f32[12,512,1024]{2,1,0:T(8,128)}, u32[]{:S(2)}) copy-start(f32[12,512,1024]{2,1,0:T(8,128)} %get-tuple-element.466) | copy-start | bytes 75497472 | tf_op jit(solution)/shard_map/while
  136.8 23.0 %copy-start.19 = (bf16[1,1024,12,64]{1,3,2,0:T(8,128)(2,1)S(1)}, bf16[1,1024,12,64]{1,3,2,0:T(8,128)(2,1)}, u32[]{:S(2)}) copy-start(bf16[1,1024,12,64]{1,3,2,0:T(8,128)(2,1)} %get-tuple-element.514) | copy-start | bytes 4718596 | tf_op jit(solution)/shard_map/while
  147.5 15.7 %copy-start = (f32[12,512,1024]{2,1,0:T(8,128)S(1)}, f32[12,512,1024]{2,1,0:T(8,128)}, u32[]{:S(2)}) copy-start(f32[12,512,1024]{2,1,0:T(8,128)} %get-tuple-element.466) | copy-start | bytes 75497472 | tf_op jit(solution)/shard_map/while
  171.9 5.3 copy-start.2
  171.9 5.2 copy-start.22
  171.9 5.2 copy-start.9
  214.1 84.1 %copy-start.18 = (bf16[1536,768]{1,0:T(8,128)(2,1)S(1)}, bf16[1536,768]{1,0:T(8,128)(2,1)}, u32[]{:S(2)}) copy-start(bf16[1536,768]{1,0:T(8,128)(2,1)} %gather_fusion) | copy-start | bytes 7077892
  326.5 14.6 %copy-start.17 = (bf16[1536,768]{1,0:T(8,128)(2,1)S(1)}, bf16[1536,768]{1,0:T(8,128)(2,1)}, u32[]{:S(2)}) copy-start(bf16[1536,768]{1,0:T(8,128)(2,1)} %gather_fusion.2) | copy-start | bytes 7077892
  440.5 654.2 %reduce-scatter.5.cloned.1.call-start = ((), (), s32[]{:S(2)}) async-start(), calls=%async_computation.7 | async-start | bytes 2433024 | tf_op jit(solution)/shard_map/reduce_scatter | solution.py:227
  482.0 8.4 copy-start.25
  482.0 8.4 copy-start.31
  482.0 8.4 copy-start.33
  490.5 5.0 copy-start.41
  490.5 5.0 copy-start.4
  490.5 5.7 copy-start.7
  496.2 4.1 copy-start.12
  500.3 2.9 copy-start.20
  506.0 4.5 copy-start.23
  506.0 714.0 %reduce-scatter.3.cloned.1.call-start = ((), (), s32[]{:S(2)}) async-start(), calls=%async_computation.6 | async-start | bytes 7299072 | tf_op jit(solution)/shard_map/reduce_scatter | solution.py:226
  515.2 14.4 %copy-start.1 = (pred[512,1024]{1,0:T(8,128)(4,1)}, pred[512,1024]{1,0:T(8,128)(4,1)S(1)}, u32[]{:S(2)}) copy-start(pred[512,1024]{1,0:T(8,128)(4,1)S(1)} %fusion.135) | copy-start | bytes 1572868 | tf_op jit(solution)/shard_map/while/body/eval_jaxpr/while
  515.2 14.4 %copy-start.14 = (bf16[1,1024,12,64]{1,3,2,0:T(8,128)(2,1)S(1)}, bf16[1,1024,12,64]{1,3,2,0:T(8,128)(2,1)}, u32[]{:S(2)}) copy-start(bf16[1,1024,12,64]{1,3,2,0:T(8,128)(2,1)} %get-tuple-element.561) | copy-start | bytes 4718596 | tf_op jit(solution)/shard_map/while/body/eval_jaxpr/while
  609.4 14.3 %copy-start.1 = (pred[512,1024]{1,0:T(8,128)(4,1)}, pred[512,1024]{1,0:T(8,128)(4,1)S(1)}, u32[]{:S(2)}) copy-start(pred[512,1024]{1,0:T(8,128)(4,1)S(1)} %fusion.135) | copy-start | bytes 1572868 | tf_op jit(solution)/shard_map/while/body/eval_jaxpr/while
  609.4 14.3 %copy-start.14 = (bf16[1,1024,12,64]{1,3,2,0:T(8,128)(2,1)S(1)}, bf16[1,1024,12,64]{1,3,2,0:T(8,128)(2,1)}, u32[]{:S(2)}) copy-start(bf16[1,1024,12,64]{1,3,2,0:T(8,128)(2,1)} %get-tuple-element.561) | copy-start | bytes 4718596 | tf_op jit(solution)/shard_map/while/body/eval_jaxpr/while
  706.2 2.6 copy-start.15
  708.8 2.8 copy-start.10
  708.8 2.8 copy-start.29
  708.9 2.7 copy-start.35
  708.9 2.7 copy-start.37
  708.9 2.7 copy-start.51
  709.5 2.1 copy-start.16
  718.4 7.9 copy-start.39
  718.4 7.9 copy-start.11
  726.2 44.0 %copy-start.6 = (f32[1024,768]{1,0:T(8,128)S(1)}, f32[1024,768]{1,0:T(8,128)}, u32[]{:S(2)}) copy-start(f32[1024,768]{1,0:T(8,128)} %copy-done.5) | copy-start | bytes 9437188
  726.3 44.0 %copy-start.44 = (f32[1024]{0:T(1024)S(1)}, f32[1024]{0:T(1024)}, u32[]{:S(2)}) copy-start(f32[1024]{0:T(1024)} %copy-done.43) | copy-start | bytes 12292
  (15 other events, 20.9 us)
Sparse Core Ops, SparseCore 0:
  10.9 62.8 all-gather.4
  76.7 52.7 all-gather.6
  133.1 80.9 all-gather.10
  217.5 80.6 all-gather.8
  440.6 549.3 all-reduce.14
  995.7 98.9 reduce-scatter.4
  1101.9 118.0 reduce-scatter.2
where the time goes:
time: 1230 us
  waiting for transfers between devices  539 us (44%)
  matrix products  308 us (25%)
  local copies, waits for them, and re-layouts  143 us (12%)
  other arithmetic  129 us (10%)
  blocking collectives  82.1 us (7%)
  between operations  15 us (1%)
    unnamed x8, waiting for transfers between devices  217 us
    reduce_scatter x1, waiting for transfers between devices, body(): lax.psum_scatter(grad_joint, ('dp', 'fsdp'), scatter_dimension=0, tiled=T...  125 us
    reduce_scatter x1, waiting for transfers between devices, body(): lax.psum_scatter(grad_proj, ('dp', 'fsdp'), scatter_dimension=0, tiled=True)  102 us
    unnamed x2, blocking collectives  82.1 us
    all_gather x1, waiting for transfers between devices, body(): piece_in = lax.all_gather(expert_in, ('dp', 'fsdp'), axis=0, tiled=True)  69.5 us
    another operation x1, local copies, waits for them, and re-layouts, body(): jnp.stack([grad_in_part, grad_out_part], 1)  55.4 us
    dot_general x4, matrix products, masked_scores(): jnp.einsum('qhd,khd->hqk', queries, keys_seq, preferred_element_type=jnp....  49.9 us
    convert_element_type x2, other arithmetic, block_back(): dscores = (probs_raw * (dprobs - delta)).astype(jnp.bfloat16)  47.2 us
  transfers between devices with their start and end apart: 7, of which 5 were waited for; matrix products, arithmetic and copies ran while one was open for 35% of the time, Pallas kernels for 0%

commit v1 on v0

v1 whole, which is shorter than its diff:
```python
import functools

import jax
import jax.numpy as jnp
from jax import lax
from jax.experimental import pallas as pl
from jax.experimental.pallas import tpu as pltpu
from jax.sharding import PartitionSpec as P

HEAD_DIM = 64
CAP = 768
TILE = 256
PAIR = 128
epsilon = 1e-05
masked_score = -1e30
gelu_coeff = 0.7978845608028654
MESH = pl.DeviceIdType.MESH
F32 = jnp.float32
BF16 = jnp.bfloat16
NT = (((1,), (1,)), ((), ()))
TN = (((0,), (0,)), ((), ()))
VMEM_BYTES = 60 * 1024 * 1024


def dot(left, right):
    return jnp.dot(left, right, preferred_element_type=F32)


def dot_nt(left, right):
    return lax.dot_general(left, right, NT, preferred_element_type=F32)


def dot_tn(left, right):
    return lax.dot_general(left, right, TN, preferred_element_type=F32)


def norm_parts(values):
    average = jnp.mean(values, axis=-1, keepdims=True)
    centered = values - average
    variance = jnp.mean(centered * centered, axis=-1, keepdims=True)
    inverse = lax.rsqrt(variance + epsilon)
    return centered * inverse, inverse


def norm_back(grad, normal, inverse, gain):
    weighted = grad * gain
    first = jnp.mean(weighted, axis=-1, keepdims=True)
    second = jnp.mean(weighted * normal, axis=-1, keepdims=True)
    return inverse * (weighted - first - normal * second)


class Cube:
    def __init__(self, dp_size, fsdp_size):
        self.dp_size, self.fsdp_size = dp_size, fsdp_size
        self.count = dp_size * fsdp_size
        self.dp_bits = [("dp", b) for b in reversed(range(dp_size.bit_length() - 1))]
        self.fsdp_bits = [("fsdp", b) for b in reversed(range(1, fsdp_size.bit_length() - 1))]
        self.core = [("fsdp", 0)]
        self.orders = (
            self.dp_bits + self.fsdp_bits + self.core,
            self.dp_bits + self.fsdp_bits[::-1] + self.core,
            self.fsdp_bits + self.dp_bits + self.core,
        )

    def here(self):
        return lax.axis_index("dp"), lax.axis_index("fsdp")

    def partner(self, where, bit):
        axis, b = bit
        dp, fsdp = where
        if axis == "dp":
            return dp + self.step(dp, b), fsdp
        return dp, fsdp + self.step(fsdp, b)

    def step(self, value, b):
        return (1 << b) * (1 - 2 * lax.rem(lax.div(value, 1 << b), 2))

    def index(self, where, order, rel):
        dp, fsdp = where
        total = dp * self.fsdp_size + fsdp
        for k, (axis, b) in enumerate(order):
            if rel >> k & 1:
                total += self.step(dp, b) * self.fsdp_size if axis == "dp" else self.step(fsdp, b)
        return total

    def greet(self, where):
        barrier = pltpu.get_barrier_semaphore()
        bits = self.dp_bits + self.fsdp_bits + self.core
        for bit in bits:
            pl.semaphore_signal(
                barrier, inc=1, device_id=self.partner(where, bit), device_id_type=MESH
            )
        pl.semaphore_wait(barrier, len(bits))


class Gather:
    def __init__(self, cube, where, order, source, place, send_sems, recv_sems, own_sem):
        self.cube, self.where, self.order = cube, where, order
        self.source, self.place = source, place
        self.send_sems, self.recv_sems, self.own_sem = send_sems, recv_sems, own_sem
        self.levels = len(order)

    def copy(self, rel, k):
        target = rel | 1 << k
        index = self.cube.index(self.where, self.order, rel)
        return pltpu.make_async_remote_copy(
            src_ref=self.source if rel == 0 else self.place(index),
            dst_ref=self.place(index),
            send_sem=self.send_sems.at[target],
            recv_sem=self.recv_sems.at[target],
            device_id=self.cube.partner(self.where, self.order[k]),
            device_id_type=MESH,
        )

    def own(self):
        return pltpu.make_async_copy(
            self.source, self.place(self.cube.index(self.where, self.order, 0)), self.own_sem
        )

    def send_on(self, rel):
        for k in range(rel.bit_length(), self.levels):
            self.copy(rel, k).start()

    def arrive(self, rel):
        k = rel.bit_length() - 1
        self.copy(rel ^ 1 << k, k).wait_recv()

    def sent(self, rel):
        k = rel.bit_length() - 1
        self.copy(rel ^ 1 << k, k).wait_send()


def gather_kernel(cube, cuts, small, large, small_all, large_all, *sems):
    where = cube.here()
    cube.greet(where)
    flows = []
    spots = [("s", lo, hi, order) for lo, hi, order in cuts] + [("l", 0, 0, 0), ("l", 1, 1, 1)]
    for number, (kind, lo, hi, order) in enumerate(spots):
        send, recv, own = sems[3 * number : 3 * number + 3]
        if kind == "s":
            source = small.at[:, lo:hi]
            place = lambda index, lo=lo, hi=hi: small_all.at[index, :, lo:hi]
        else:
            source = large.at[lo]
            place = lambda index, lo=lo: large_all.at[index, lo]
        flows.append(Gather(cube, where, cube.orders[order], source, place, send, recv, own))
    groups = (flows[: len(cuts)], flows[len(cuts) :])
    for group in groups:
        for flow in group:
            flow.send_on(0)
            flow.own().start()
    for group in groups:
        for rel in range(1, cube.count):
            for flow in group:
                flow.arrive(rel)
                flow.send_on(rel)
    for flow in flows:
        flow.own().wait()
        for rel in range(1, cube.count):
            flow.sent(rel)


def gather_all(cube, small, large):
    count = cube.count
    columns = small.shape[1]
    lanes = columns // 128
    first, second = 128 * (lanes * 2 // 5), 128 * (lanes * 4 // 5)
    cuts = ((0, first, 0), (first, second, 1), (second, columns, 2))
    sems = []
    for _ in range(len(cuts) + 2):
        sems += [
            pltpu.SemaphoreType.DMA((count,)),
            pltpu.SemaphoreType.DMA((count,)),
            pltpu.SemaphoreType.DMA,
        ]
    return pl.pallas_call(
        functools.partial(gather_kernel, cube, cuts),
        out_shape=(
            jax.ShapeDtypeStruct((count,) + small.shape, small.dtype),
            jax.ShapeDtypeStruct((count,) + large.shape, large.dtype),
        ),
        in_specs=[pl.BlockSpec(memory_space=pl.ANY)] * 2,
        out_specs=(pl.BlockSpec(memory_space=pl.ANY),) * 2,
        scratch_shapes=sems,
        compiler_params=pltpu.CompilerParams(collective_id=0, has_side_effects=True),
    )(small, large)


class Reduce:
    def __init__(self, cube, where, order, part, kept, slot, send_sems, recv_sems, own_sems):
        self.cube, self.where, self.order = cube, where, order
        self.part, self.kept, self.slot = part, kept, slot
        self.send_sems, self.recv_sems, self.own_sems = send_sems, recv_sems, own_sems
        self.levels = len(order)
        self.half = cube.count // 2

    def copy(self, rel):
        k = rel.bit_length() - 1
        if rel >= self.half:
            source = self.part(self.cube.index(self.where, self.order, rel))
        else:
            source = self.kept(rel)
        return pltpu.make_async_remote_copy(
            src_ref=source,
            dst_ref=self.slot(rel),
            send_sem=self.send_sems.at[rel],
            recv_sem=self.recv_sems.at[rel],
            device_id=self.cube.partner(self.where, self.order[k]),
            device_id_type=MESH,
        )

    def own(self, rel):
        return pltpu.make_async_copy(
            self.part(self.cube.index(self.where, self.order, rel)),
            self.kept(rel),
            self.own_sems.at[rel],
        )

    def slots(self, rel):
        return [rel | 1 << k for k in range(rel.bit_length(), self.levels)]


def reduce_kernel(cube, cuts, parts, total, kept, slots, *sems):
    where = cube.here()
    cube.greet(where)
    flows = []
    for number, (lo, hi, order) in enumerate(cuts):
        send, recv, own = sems[3 * number : 3 * number + 3]
        flows.append(
            (
                lo,
                hi,
                Reduce(
                    cube,
                    where,
                    cube.orders[order],
                    lambda index, lo=lo, hi=hi: parts.at[index, :, :, lo:hi],
                    lambda rel, lo=lo, hi=hi: kept.at[rel, :, :, lo:hi],
                    lambda rel, lo=lo, hi=hi: slots.at[rel, :, :, lo:hi],
                    send,
                    recv,
                    own,
                ),
            )
        )
    half = cube.count // 2
    for rel in reversed(range(cube.count)):
        for _, _, flow in flows:
            if rel >= half:
                flow.copy(rel).start()
            else:
                flow.own(rel).start()
    units = kept.shape[1]
    for rel in reversed(range(half)):
        for lo, hi, flow in flows:
            flow.own(rel).wait()
            sources = flow.slots(rel)
            for other in sources:
                flow.copy(other).wait_recv()

            def add(unit, carry):
                value = kept[rel, unit, :, lo:hi].astype(F32)
                for other in sources:
                    value += slots[other, unit, :, lo:hi].astype(F32)
                if rel:
                    kept[rel, unit, :, lo:hi] = value.astype(BF16)
                else:
                    total[unit, :, lo:hi] = value
                return carry

            lax.fori_loop(0, units, add, 0)
            if rel:
                flow.copy(rel).start()
    for _, _, flow in flows:
        for rel in range(1, cube.count):
            flow.copy(rel).wait_send()


def reduce_all(cube, parts, cuts, collective_id):
    count = cube.count
    block = parts.shape[1:]
    sems = []
    for _ in cuts:
        sems += [pltpu.SemaphoreType.DMA((count,))] * 2
        sems += [pltpu.SemaphoreType.DMA((count // 2,))]
    return pl.pallas_call(
        functools.partial(reduce_kernel, cube, cuts),
        out_shape=jax.ShapeDtypeStruct(block, F32),
        in_specs=[pl.BlockSpec(memory_space=pl.ANY)],
        out_specs=pl.BlockSpec(memory_space=pltpu.VMEM),
        scratch_shapes=[
            pltpu.VMEM((count // 2,) + block, BF16),
            pltpu.VMEM((count,) + block, BF16),
        ]
        + sems,
        compiler_params=pltpu.CompilerParams(
            collective_id=collective_id, has_side_effects=True, vmem_limit_bytes=VMEM_BYTES
        ),
    )(parts)


def params(*semantics):
    return pltpu.CompilerParams(
        dimension_semantics=semantics or None, vmem_limit_bytes=VMEM_BYTES
    )


def norm_rows(ref):
    return jnp.transpose(ref[...].astype(F32))


def project_kernel(x_ref, w_ref, n_ref, normed_ref, joint_ref, rows):
    @pl.when(pl.program_id(0) == 0)
    def _():
        rows[...] = norm_rows(n_ref)

    normal, _ = norm_parts(x_ref[...].astype(F32))
    normed = (normal * rows[0:1] + rows[1:2]).astype(BF16)
    normed_ref[...] = normed
    joint_ref[...] = dot(normed, w_ref[...]).astype(BF16)


def project(inputs, whole):
    tokens, width = inputs.shape
    return pl.pallas_call(
        project_kernel,
        grid=(tokens // TILE,),
        out_shape=(
            jax.ShapeDtypeStruct((tokens, width), BF16),
            jax.ShapeDtypeStruct((tokens, 3 * width), BF16),
        ),
        in_specs=[
            pl.BlockSpec((TILE, width), lambda i: (i, 0)),
            pl.BlockSpec((width, 3 * width), lambda i: (0, 0)),
            pl.BlockSpec((width, 128), lambda i: (0, 4 * width // 128)),
        ],
        out_specs=(
            pl.BlockSpec((TILE, width), lambda i: (i, 0)),
            pl.BlockSpec((TILE, 3 * width), lambda i: (i, 0)),
        ),
        scratch_shapes=[pltpu.VMEM((128, width), F32)],
        compiler_params=params("arbitrary"),
    )(inputs, whole, whole)


def lane_iota(shape):
    return lax.broadcasted_iota(jnp.int32, shape, 1)


def row_iota(shape):
    return lax.broadcasted_iota(jnp.int32, shape, 0)


def attend_kernel(len_ref, q_ref, k_ref, v_ref, mixed_ref, lse_ref, keys):
    pair = pl.program_id(0)
    length = q_ref.shape[0]
    valid = len_ref[0]
    lane = lane_iota((length, PAIR))
    bias = jnp.where((lane == 0) & (row_iota((length, PAIR)) >= valid), masked_score, 0.0)
    keys[:, :PAIR] = k_ref[...]
    keys[:, PAIR:] = bias.astype(BF16)
    lane = lane_iota((TILE, PAIR))
    upper = lane_iota((TILE, TILE)) > row_iota((TILE, TILE))
    ones = jnp.where(lane == 0, 1.0, 0.0).astype(BF16)

    @pl.when(pair == 0)
    def _():
        lse_ref[...] = jnp.zeros_like(lse_ref)

    for block in range(length // TILE):
        rows = pl.ds(block * TILE, TILE)
        outs = []
        marks = lse_ref[rows, :]
        for head in range(2):
            mine = (lane >= head * HEAD_DIM) & (lane < (head + 1) * HEAD_DIM)
            query = jnp.where(mine, q_ref[rows, :].astype(F32) * HEAD_DIM**-0.5, 0.0).astype(BF16)
            query = jnp.concatenate([query, ones], axis=1)
            near = dot_nt(query, keys[rows, :])
            near = jnp.where(upper, masked_score, near)
            top = jnp.max(near, axis=-1, keepdims=True)
            if block:
                far = dot_nt(query, keys[: block * TILE, :])
                top = jnp.maximum(top, jnp.max(far, axis=-1, keepdims=True))
            near = jnp.exp(near - top)
            total = jnp.sum(near, axis=-1, keepdims=True)
            out = dot(near.astype(BF16), v_ref[rows, :])
            if block:
                far = jnp.exp(far - top)
                total += jnp.sum(far, axis=-1, keepdims=True)
                out += dot(far.astype(BF16), v_ref[: block * TILE, :])
            outs.append(out / total)
            marks = jnp.where(lane == 2 * pair + head, top + jnp.log(total), marks)
        mixed_ref[rows, :] = jnp.where(lane < HEAD_DIM, outs[0], outs[1]).astype(BF16)
        lse_ref[rows, :] = marks


def attend(joint, lengths):
    tokens = joint.shape[0]
    width = joint.shape[1] // 3
    pairs = width // PAIR
    return pl.pallas_call(
        attend_kernel,
        grid_spec=pltpu.PrefetchScalarGridSpec(
            num_scalar_prefetch=1,
            grid=(pairs,),
            in_specs=[
                pl.BlockSpec((tokens, PAIR), lambda p, _: (0, p)),
                pl.BlockSpec((tokens, PAIR), lambda p, _: (0, pairs + p)),
                pl.BlockSpec((tokens, PAIR), lambda p, _: (0, 2 * pairs + p)),
            ],
            out_specs=(
                pl.BlockSpec((tokens, PAIR), lambda p, _: (0, p)),
                pl.BlockSpec((tokens, 128), lambda p, _: (0, 0)),
            ),
            scratch_shapes=[pltpu.VMEM((tokens, 2 * PAIR), BF16)],
        ),
        out_shape=(
            jax.ShapeDtypeStruct((tokens, width), BF16),
            jax.ShapeDtypeStruct((tokens, 128), F32),
        ),
        compiler_params=params("arbitrary"),
    )(lengths, joint, joint, joint)


def middle_kernel(x_ref, mixed_ref, w_ref, n_ref, place_ref, residual_ref, slots_ref, normed, rows):
    rows[...] = norm_rows(n_ref)
    tokens = x_ref.shape[0]
    for start in range(0, tokens, TILE):
        part = pl.ds(start, TILE)
        residual = x_ref[part, :].astype(F32) + dot(mixed_ref[part, :], w_ref[...])
        residual_ref[part, :] = residual
        normal, _ = norm_parts(residual)
        normed[part, :] = (normal * rows[2:3] + rows[3:4]).astype(BF16)
    for start in range(0, slots_ref.shape[0], TILE):
        part = pl.ds(start, TILE)
        slots_ref[part, :] = dot(place_ref[part, :], normed[...]).astype(BF16)


def middle(inputs, mixed, whole, place):
    tokens, width = inputs.shape
    full = lambda shape: pl.BlockSpec(shape, lambda i: (0, 0))
    return pl.pallas_call(
        middle_kernel,
        grid=(1,),
        out_shape=(
            jax.ShapeDtypeStruct((tokens, width), F32),
            jax.ShapeDtypeStruct((place.shape[0], width), BF16),
        ),
        in_specs=[
            full((tokens, width)),
            full((tokens, width)),
            pl.BlockSpec((width, width), lambda i: (0, 3)),
            pl.BlockSpec((width, 128), lambda i: (0, 4 * width // 128)),
            full(place.shape),
        ],
        out_specs=(full((tokens, width)), full((place.shape[0], width))),
        scratch_shapes=[pltpu.VMEM((tokens, width), BF16), pltpu.VMEM((128, width), F32)],
        compiler_params=params("arbitrary"),
    )(inputs, mixed, whole, whole, place)


def expert_kernel(owner, x_ref, g_ref, w_ref, out_ref, back_ref, grads_ref, in_acc, out_acc):
    step = pl.program_id(0)
    groups, _, experts, rows, width = w_ref.shape
    hidden = groups * rows
    tiles = x_ref.shape[0] // TILE

    @pl.when(step == 0)
    def _():
        out_ref[...] = jnp.zeros_like(out_ref)
        back_ref[...] = jnp.zeros_like(back_ref)

    in_acc[...] = jnp.zeros_like(in_acc)
    out_acc[...] = jnp.zeros_like(out_acc)

    def tile_step(tile, carry):
        expert = owner[tile]
        part = pl.ds(pl.multiple_of(tile * TILE, TILE), TILE)
        w_in = w_ref[:, 0, expert].reshape(hidden, width)
        w_out = w_ref[:, 1, expert].reshape(hidden, width)
        tokens = x_ref[part, :]
        cotangent = g_ref[part, :]
        pre = dot_nt(w_in, tokens)
        dact = dot_nt(w_out, cotangent)
        square = pre * pre
        bend = jnp.tanh(gelu_coeff * pre * (1.0 + 0.044715 * square))
        lift = 0.5 * (1.0 + bend)
        act = (pre * lift).astype(BF16)
        slope = lift + 0.5 * pre * (1.0 - bend * bend) * gelu_coeff * (1.0 + 0.134145 * square)
        dpre = (slope * dact).astype(BF16)
        in_acc[expert] += dot(dpre, tokens)
        out_acc[expert] += dot(act, cotangent)
        out_ref[part, :] += dot_tn(act, w_out)
        back_ref[part, :] += dot_tn(dpre, w_in)
        return carry

    lax.fori_loop(0, tiles, tile_step, 0)
    for expert in range(experts):
        grads_ref[:, 0, expert] = in_acc[expert].astype(BF16).reshape(groups, rows, width)
        grads_ref[:, 1, expert] = out_acc[expert].astype(BF16).reshape(groups, rows, width)


def run_experts(owner, slot_inputs, slot_grads, weights):
    count, _, experts, rows, width = weights.shape
    slots = slot_inputs.shape[0]
    groups = max(1, 384 // rows)
    block = (groups,) + weights.shape[1:]
    full = pl.BlockSpec((slots, width), lambda i, _: (0, 0))
    piece = pl.BlockSpec(block, lambda i, _: (i, 0, 0, 0, 0))
    return pl.pallas_call(
        expert_kernel,
        grid_spec=pltpu.PrefetchScalarGridSpec(
            num_scalar_prefetch=1,
            grid=(count // groups,),
            in_specs=[full, full, piece],
            out_specs=(full, full, piece),
            scratch_shapes=[pltpu.VMEM((experts, groups * rows, width), F32)] * 2,
        ),
        out_shape=(
            jax.ShapeDtypeStruct((slots, width), F32),
            jax.ShapeDtypeStruct((slots, width), F32),
            jax.ShapeDtypeStruct(weights.shape, BF16),
        ),
        compiler_params=params("arbitrary"),
    )(owner, slot_inputs, slot_grads, weights)


def split(values):
    high = values.astype(BF16)
    return high, (values - high.astype(F32)).astype(BF16)


def turn_kernel(
    out_ref, back_ref, place_ref, residual_ref, mixed_ref, grad_ref, w_ref, n_ref,
    hidden_ref, dres_ref, dproj_ref, dmixed_ref, delta_ref, wgrad_ref, ngrad_ref, rows,
):
    step = pl.program_id(0)
    width = residual_ref.shape[1]

    @pl.when(step == 0)
    def _():
        rows[...] = norm_rows(n_ref)
        wgrad_ref[...] = jnp.zeros_like(wgrad_ref)
        ngrad_ref[...] = jnp.zeros_like(ngrad_ref)

    place = place_ref[...]
    branch = dot_tn(place, out_ref[...].astype(BF16))
    dnormed = dot_tn(place, back_ref[...].astype(BF16))
    residual = residual_ref[...]
    hidden_ref[...] = (residual + branch).astype(BF16)
    normal, inverse = norm_parts(residual)
    ngrad_ref[0:1] += jnp.sum(dnormed * normal, axis=0, keepdims=True)
    ngrad_ref[1:2] += jnp.sum(dnormed, axis=0, keepdims=True)
    dres = grad_ref[...].astype(F32) + norm_back(dnormed, normal, inverse, rows[2:3])
    dres_ref[...] = dres
    dproj = dres.astype(BF16)
    mixed = mixed_ref[...]
    wgrad_ref[...] += dot_tn(mixed, dproj)
    dmixed = dot_nt(dproj, w_ref[...]).astype(BF16)
    dmixed_ref[...] = dmixed
    heads = (row_iota((width, 128)) // HEAD_DIM == lane_iota((width, 128))).astype(BF16)
    high, low = split(dmixed.astype(F32) * mixed.astype(F32))
    delta_ref[...] = dot(high, heads) + dot(low, heads)


def turn(out, back, place, residual, mixed, grad, whole):
    tokens, width = residual.shape
    slots = out.shape[0]
    row = pl.BlockSpec((TILE, width), lambda i: (i, 0))
    full = lambda shape, *at: pl.BlockSpec(shape, lambda i: at or (0, 0))
    return pl.pallas_call(
        turn_kernel,
        grid=(tokens // TILE,),
        out_shape=(
            jax.ShapeDtypeStruct((tokens, width), BF16),
            jax.ShapeDtypeStruct((tokens, width), F32),
            jax.ShapeDtypeStruct((tokens, width), BF16),
            jax.ShapeDtypeStruct((tokens, width), BF16),
            jax.ShapeDtypeStruct((tokens, 128), F32),
            jax.ShapeDtypeStruct((width, width), F32),
            jax.ShapeDtypeStruct((8, width), F32),
        ),
        in_specs=[
            full((slots, width)),
            full((slots, width)),
            pl.BlockSpec((slots, TILE), lambda i: (0, i)),
            row,
            row,
            row,
            full((width, width), 0, 3),
            full((width, 128), 0, 4 * width // 128),
        ],
        out_specs=(
            row, row, row, row,
            pl.BlockSpec((TILE, 128), lambda i: (i, 0)),
            full((width, width)),
            full((8, width)),
        ),
        scratch_shapes=[pltpu.VMEM((128, width), F32)],
        compiler_params=params("arbitrary"),
    )(out, back, place, residual, mixed, grad, whole, whole)


def column(values, at):
    return jnp.sum(jnp.where(lane_iota(values.shape) == at, values, 0.0), axis=1, keepdims=True)


def extra_lanes(values, more=None):
    high = values.astype(BF16).astype(F32)
    mid = (values - high).astype(BF16).astype(F32)
    low = values - high - mid
    lane = lane_iota((values.shape[0], PAIR))
    out = jnp.where(lane == 0, high, jnp.where(lane == 1, mid, jnp.where(lane == 2, low, 0.0)))
    if more is not None:
        out = jnp.where(lane == 3, more, out)
    return out.astype(BF16)


def attend_back_kernel(
    len_ref, q_ref, k_ref, v_ref, d_ref, lse_ref, delta_ref, dq_ref, dk_ref, dv_ref,
    keys, values, queries, grads, dq_acc,
):
    pair = pl.program_id(0)
    length = q_ref.shape[0]
    valid = len_ref[0]
    lane = lane_iota((length, PAIR))
    late = row_iota((length, PAIR)) >= valid
    marks = jnp.where(lane < 3, 1.0, jnp.where((lane == 3) & late, masked_score, 0.0))
    keys[:, :PAIR] = k_ref[...]
    keys[:, PAIR:] = marks.astype(BF16)
    values[:, :PAIR] = v_ref[...]
    values[:, PAIR:] = jnp.where(lane < 3, 1.0, 0.0).astype(BF16)
    key_rows = jnp.transpose(k_ref[...])
    scaled = (q_ref[...].astype(F32) * HEAD_DIM**-0.5).astype(BF16)
    lower = row_iota((TILE, TILE)) > lane_iota((TILE, TILE))
    half = lane_iota((TILE, PAIR)) < HEAD_DIM
    dq_acc[...] = jnp.zeros_like(dq_acc)
    for head in range(2):
        mine = (lane >= head * HEAD_DIM) & (lane < (head + 1) * HEAD_DIM)
        queries[head, :, :PAIR] = jnp.where(mine, scaled.astype(F32), 0.0).astype(BF16)
        queries[head, :, PAIR:] = extra_lanes(-column(lse_ref[...], 2 * pair + head), 1.0)
        grads[head, :, :PAIR] = jnp.where(mine, d_ref[...].astype(F32), 0.0).astype(BF16)
        grads[head, :, PAIR:] = extra_lanes(-column(delta_ref[...], 2 * pair + head))
    for block in range(length // TILE):
        rows = pl.ds(block * TILE, TILE)
        dks, dvs = [], []
        for head in range(2):
            dk = dv = None
            for start in range(block * TILE, length, TILE):
                later = pl.ds(start, TILE)
                scores = dot_nt(keys[rows, :], queries[head, later, :])
                if start == block * TILE:
                    scores = jnp.where(lower, masked_score, scores)
                probs = jnp.exp(scores)
                dscores = probs * dot_nt(values[rows, :], grads[head, later, :])
                probs, dscores = probs.astype(BF16), dscores.astype(BF16)
                more_v = dot(probs, grads[head, later, :PAIR])
                more_k = dot(dscores, queries[head, later, :PAIR])
                dv = more_v if dv is None else dv + more_v
                dk = more_k if dk is None else dk + more_k
                spot = pl.ds(head * HEAD_DIM, HEAD_DIM)
                dq_acc[spot, start : start + TILE] += dot(
                    key_rows[head * HEAD_DIM : (head + 1) * HEAD_DIM, block * TILE : (block + 1) * TILE],
                    dscores,
                )
            dks.append(dk)
            dvs.append(dv)
        dk_ref[rows, :] = jnp.where(half, dks[0], dks[1]).astype(BF16)
        dv_ref[rows, :] = jnp.where(half, dvs[0], dvs[1]).astype(BF16)
    dq_ref[...] = jnp.transpose(dq_acc[...] * HEAD_DIM**-0.5).astype(BF16)


def attend_back(joint, dmixed, lse, delta, lengths):
    tokens, width = dmixed.shape
    pairs = width // PAIR
    narrow = pl.BlockSpec((tokens, PAIR), lambda p, _: (0, p))
    full = pl.BlockSpec((tokens, 128), lambda p, _: (0, 0))
    return pl.pallas_call(
        attend_back_kernel,
        grid_spec=pltpu.PrefetchScalarGridSpec(
            num_scalar_prefetch=1,
            grid=(pairs,),
            in_specs=[
                narrow,
                pl.BlockSpec((tokens, PAIR), lambda p, _: (0, pairs + p)),
                pl.BlockSpec((tokens, PAIR), lambda p, _: (0, 2 * pairs + p)),
                narrow,
                full,
                full,
            ],
            out_specs=(narrow,) * 3,
            scratch_shapes=[
                pltpu.VMEM((tokens, 2 * PAIR), BF16),
                pltpu.VMEM((tokens, 2 * PAIR), BF16),
                pltpu.VMEM((2, tokens, 2 * PAIR), BF16),
                pltpu.VMEM((2, tokens, 2 * PAIR), BF16),
                pltpu.VMEM((PAIR, tokens), F32),
            ],
        ),
        out_shape=(jax.ShapeDtypeStruct((tokens, width), BF16),) * 3,
        compiler_params=params("arbitrary"),
    )(lengths, joint, joint, joint, dmixed, lse, delta)


def finish_kernel(
    dq_ref, dk_ref, dv_ref, normed_ref, w_ref, n_ref, x_ref, dres_ref, wgrad_ref, ngrad_ref,
    input_ref, pack_ref, rows, acc, sums,
):
    step = pl.program_id(0)
    width = x_ref.shape[1]

    @pl.when(step == 0)
    def _():
        rows[...] = norm_rows(n_ref)
        acc[...] = jnp.zeros_like(acc)
        sums[...] = jnp.zeros_like(sums)
        sums[2:4, :] = ngrad_ref[0:2, :]

    normed = normed_ref[...]
    dnormed = None
    for number, ref in enumerate((dq_ref, dk_ref, dv_ref)):
        part = slice(number * width, (number + 1) * width)
        value = ref[...]
        more = dot_nt(value, w_ref[:, part])
        dnormed = more if dnormed is None else dnormed + more
        acc[:, part] += dot_tn(normed, value)
    normal, inverse = norm_parts(x_ref[...].astype(F32))
    sums[0:1] += jnp.sum(dnormed * normal, axis=0, keepdims=True)
    sums[1:2] += jnp.sum(dnormed, axis=0, keepdims=True)
    input_ref[...] = (dres_ref[...] + norm_back(dnormed, normal, inverse, rows[0:1])).astype(BF16)

    @pl.when(step == pl.num_programs(0) - 1)
    def _():
        pack_ref[:, : 3 * width] = acc[...].astype(BF16)
        pack_ref[:, 3 * width : 4 * width] = wgrad_ref[...].astype(BF16)
        pack_ref[:, 4 * width :] = jnp.transpose(sums[...]).astype(BF16)


def finish(dqkv, normed, whole, inputs, dres, wgrad, ngrad):
    tokens, width = inputs.shape
    row = pl.BlockSpec((TILE, width), lambda i: (i, 0))
    full = lambda shape, *at: pl.BlockSpec(shape, lambda i: at or (0, 0))
    return pl.pallas_call(
        finish_kernel,
        grid=(tokens // TILE,),
        out_shape=(
            jax.ShapeDtypeStruct((tokens, width), BF16),
            jax.ShapeDtypeStruct((width, 4 * width + 128), BF16),
        ),
        in_specs=[
            row, row, row, row,
            full((width, 3 * width)),
            full((width, 128), 0, 4 * width // 128),
            row, row,
            full((width, width)),
            full((8, width)),
        ],
        out_specs=(row, full((width, 4 * width + 128))),
        scratch_shapes=[
            pltpu.VMEM((128, width), F32),
            pltpu.VMEM((width, 3 * width), F32),
            pltpu.VMEM((128, width), F32),
        ],
        compiler_params=params("arbitrary"),
    )(*dqkv, normed, whole, whole, inputs, dres, wgrad, ngrad)


def route(chosen, tokens):
    slots = tokens + TILE
    second = chosen.astype(jnp.int32)
    ones = jnp.cumsum(second)
    zeros = jnp.cumsum(1 - second)
    edge = (zeros[-1] + TILE - 1) // TILE * TILE
    spot = jnp.where(second == 0, zeros - 1, edge + ones - 1)
    place = (jnp.arange(slots, dtype=jnp.int32)[:, None] == spot[None, :]).astype(BF16)
    owner = (jnp.arange(slots // TILE, dtype=jnp.int32) * TILE >= edge).astype(jnp.int32)
    return place, owner


def body(
    cube,
    hidden_in,
    lengths,
    expert_ids,
    norm1_gain,
    norm1_bias,
    qkv_weight,
    attn_out_weight,
    norm2_gain,
    norm2_bias,
    expert_in,
    expert_out,
    out_grad,
):
    tokens, width = hidden_in.shape
    rows = qkv_weight.shape[0]
    count = cube.count
    norms = jnp.stack([norm1_gain, norm1_bias, norm2_gain, norm2_bias], 1)
    small = jnp.concatenate(
        [qkv_weight, attn_out_weight, jnp.pad(norms, ((0, 0), (0, 124)))], axis=1
    )
    large = jnp.stack([expert_in, expert_out], 0).transpose(0, 2, 1, 3)
    small_all, large_all = gather_all(cube, small, large)
    whole = small_all.reshape(count * rows, small.shape[1])
    place, owner = route(expert_ids[:, 0], tokens)
    slot_grads = jnp.dot(place, out_grad, preferred_element_type=F32).astype(BF16)
    normed, joint = project(hidden_in, whole)
    mixed, lse = attend(joint, lengths)
    residual, slot_inputs = middle(hidden_in, mixed, whole, place)
    out, back, grads = run_experts(owner, slot_inputs, slot_grads, large_all)
    shape = (count, 4, grads.shape[3], width)
    expert_total = reduce_all(
        cube,
        grads.reshape(shape),
        ((0, width // 2, 0), (width // 2, width, 1)),
        1,
    ).reshape(grads.shape[1:])
    hidden_out, dres, dproj, dmixed, delta, wgrad, ngrad = turn(
        out, back, place, residual, mixed, out_grad, whole
    )
    dqkv = attend_back(joint, dmixed, lse, delta, lengths)
    input_grad, pack = finish(dqkv, normed, whole, hidden_in, dres, wgrad, ngrad)
    columns = pack.shape[1]
    lanes = columns // 128
    first, second = 128 * (lanes * 2 // 5), 128 * (lanes * 4 // 5)
    total = reduce_all(
        cube,
        pack.reshape(count, 1, rows, columns),
        ((0, first, 0), (first, second, 1), (second, columns, 2)),
        2,
    )[0]
    return (
        hidden_out,
        input_grad,
        total[:, 4 * width],
        total[:, 4 * width + 1],
        total[:, : 3 * width],
        total[:, 3 * width : 4 * width],
        total[:, 4 * width + 2],
        total[:, 4 * width + 3],
        expert_total[0].transpose(1, 0, 2),
        expert_total[1].transpose(1, 0, 2),
    )


def solution(mesh):
    cube = Cube(mesh.shape["dp"], mesh.shape["fsdp"])
    both = ("dp", "fsdp")
    vector, matrix, cube3 = P(both), P(both, None), P(both, None, None)
    in_specs = (
        matrix, vector, matrix, vector, vector, matrix, matrix, vector, vector, cube3, cube3, matrix,
    )
    out_specs = (
        matrix, matrix, vector, vector, matrix, matrix, vector, vector, cube3, cube3,
    )
    return jax.shard_map(
        functools.partial(body, cube),
        mesh=mesh,
        in_specs=in_specs,
        out_specs=out_specs,
        check_vma=False,
    )
```

time: 1230 us -> 469 us (0.38)
  waiting for transfers between devices: 539 us -> 0 us
  Pallas kernels: 0 us -> 442 us
  matrix products: 308 us -> 3.68 us
  local copies, waits for them, and re-layouts: 143 us -> 10.8 us
  other arithmetic: 129 us -> 9.27 us
  blocking collectives: 82.1 us -> 0 us
  between operations: 15 us -> 2.14 us
    pallas_call x0 -> x10, Pallas kernels: none -> 442 us  [the longest x2 136 us: reduce_all(): pl.pallas_call(functools.partial(reduce_kernel, cube, cuts), out_shape=ja...]
    dot_general x26 -> x1, matrix products: 308 us -> 3.68 us  [body(): jnp.dot(place, out_grad, preferred_element_type=F32).astype(BF16)]
    reduce_scatter x2 -> x0, waiting for transfers between devices: 227 us -> none  [the longest x1 125 us: body(): lax.psum_scatter(grad_joint, ('dp', 'fsdp'), scatter_dimension=0, tiled=T...]
    unnamed x8 -> x0, waiting for transfers between devices: 217 us -> none
    all_gather x4 -> x0, waiting for transfers between devices: 95.2 us -> none  [the longest x1 69.5 us: body(): piece_in = lax.all_gather(expert_in, ('dp', 'fsdp'), axis=0, tiled=True)]
    unnamed x2 -> x0, blocking collectives: 82.1 us -> none
    another operation x2 -> x5, local copies, waits for them, and re-layouts: 59.6 us -> 1.51 us  [the longest x1 1.11 us: body(): large = jnp.stack([expert_in, expert_out], 0).transpose(0, 2, 1, 3)]
    convert_element_type x10 -> x2, other arithmetic: 53.9 us -> 3.24 us  [the longest x1 2.73 us: route(): (jnp.arange(slots, dtype=jnp.int32)[:, None] == spot[None, :]).astype(BF16)]
  transfers between devices with their start and end apart: 7 -> 0, of which waited for: 5 -> 0; matrix products, arithmetic and copies ran while one was open for 35% -> 0% of each run, Pallas kernels for 0% -> 0%
where the time goes in v1:
time: 469 us; the launch traced here: 468 us
  Pallas kernels  442 us (94%)
  local copies, waits for them, and re-layouts  10.8 us (2%)
  other arithmetic  9.27 us (2%)
    pallas_call x2, Pallas kernels, reduce_all(): pl.pallas_call(functools.partial(reduce_kernel, cube, cuts), out_shape=ja...  136 us
    pallas_call x1, Pallas kernels, gather_all(): pl.pallas_call(functools.partial(gather_kernel, cube, cuts), out_shape=(j...  123 us
    pallas_call x1, Pallas kernels, run_experts(): pl.pallas_call(expert_kernel, grid_spec=pltpu.PrefetchScalarGridSpec(num_...  71.5 us
    pallas_call x1, Pallas kernels, attend_back(): pl.pallas_call(attend_back_kernel, grid_spec=pltpu.PrefetchScalarGridSpec...  38 us
    pallas_call x1, Pallas kernels, attend(): pl.pallas_call(attend_kernel, grid_spec=pltpu.PrefetchScalarGridSpec(num_...  23 us
    pallas_call x1, Pallas kernels, turn(): pl.pallas_call(turn_kernel, grid=(tokens // TILE,), out_shape=(jax.ShapeD...  17.1 us
    pallas_call x1, Pallas kernels, finish(): pl.pallas_call(finish_kernel, grid=(tokens // TILE,), out_shape=(jax.Shap...  16.4 us

profile of v1, /device:TPU:0, one launch (start us, length us, event | category | flops | bytes accessed | tf_op | source)
XLA Modules:
  0.0 468.1 jit_solution(17913955054941561029)
XLA Ops:
  0.6 0.0 copy-start
  1.4 0.7 pad_maximum_fusion
  2.1 0.7 compare_reduce_fusion
  2.8 1.0 reduce-window.24
  3.8 0.1 slice.46
  3.9 0.1 slice_reduce_fusion.4
  4.0 0.7 broadcast_subtract_fusion
  4.7 0.3 reduce-window.16
  5.0 0.1 slice.43
  5.1 0.1 slice_reduce_fusion.5
  5.2 0.1 add_bitcast_fusion
  5.3 0.6 slice.45
  6.6 0.1 bitcast_select_fusion
  6.6 0.5 compare_convert_fusion.owner
  7.2 0.1 copy.38
  7.2 1.6 fusion.5.small
  8.8 1.1 copy_bitcast_fusion
  10.0 0.9 maximum_bitcast_fusion.large
  10.8 0.0 copy-done
  10.8 3.7 fusion.2.g_ref
  14.5 2.7 fusion.1.place_ref
  17.2 123.0 %shard_map.195 = (bf16[32,24,3200]{2,1,0:T(8,128)(2,1)}, bf16[32,2,2,96,768]{4,3,2,1,0:T(8,128)(2,1)}) custom-call(bf16[24,3200]{1,0:T(8,128)(2,1)} %fusion.5.small, bf16[2,2,96,768]{3,2,1,0:T(8,128)(2,1)} %maximum_bitcast_fusion.large), custom_call_target="tpu_custom_call" | custom-call | tf_op jit(solution)/shard_map/pallas_call | solution.py:176
  140.3 8.8 %shard_map.196 = (bf16[1024,768]{1,0:T(8,128)(2,1)}, bf16[1024,2304]{1,0:T(8,128)(2,1)}) custom-call(bf16[1024,768]{1,0:T(8,128)(2,1)} %x_ref.5, bf16[768,3200]{1,0:T(8,128)(2,1)} %bitcast.25, bf16[768,3200]{1,0:T(8,128)(2,1)} %bitcast.26), custom_call_target="tpu_custom_call" | custom-call | tf_op jit(solution)/shard_map/pallas_call | solution.py:325
  149.1 23.0 %shard_map.197 = (bf16[1024,768]{1,0:T(8,128)(2,1)}, f32[1024,128]{1,0:T(8,128)}) custom-call(s32[1]{0:T(128)S(6)} %copy.45.len_ref, bf16[1024,2304]{1,0:T(8,128)(2,1)} %get-tuple-element.33.q_ref.k_ref.v_ref, bf16[1024,2304]{1,0:T(8,128)(2,1)} %get-tuple-element.33.q_ref.k_ref.v_ref, bf16[1024,2304]{1,0:T(8,128)(2,1)} %get-tuple-element.33.q_ref.k_ref.v_ref), custom_call_target="tpu_custom_call" | custom-call | tf_op jit(solution)/shard_map/pallas_call | solution.py:401
  172.1 8.4 %shard_map.198 = (f32[1024,768]{1,0:T(8,128)}, bf16[1280,768]{1,0:T(8,128)(2,1)}) custom-call(bf16[1024,768]{1,0:T(8,128)(2,1)} %x_ref.5, bf16[1024,768]{1,0:T(8,128)(2,1)} %get-tuple-element.34.mixed_ref, bf16[768,3200]{1,0:T(8,128)(2,1)} %bitcast.27, bf16[768,3200]{1,0:T(8,128)(2,1)} %bitcast.28, bf16[1280,1024]{1,0:T(8,128)(2,1)} %fusion.1.place_ref), custom_call_target="tpu_custom_call" | custom-call | tf_op jit(solution)/shard_map/pallas_call | solution.py:442
  180.5 71.5 %shard_map.199 = (f32[1280,768]{1,0:T(8,128)}, f32[1280,768]{1,0:T(8,128)}, bf16[32,2,2,96,768]{4,3,2,1,0:T(8,128)(2,1)}) custom-call(s32[5]{0:T(128)} %compare_convert_fusion.owner, bf16[1280,768]{1,0:T(8,128)(2,1)} %get-tuple-element.35.x_ref, bf16[1280,768]{1,0:T(8,128)(2,1)} %fusion.2.g_ref, bf16[32,2,2,96,768]{4,3,2,1,0:T(8,128)(2,1)} %get-tuple-element.36.w_ref), custom_call_target="tpu_custom_call" | custom-call | tf_op jit(solution)/shard_map/pallas_call | solution.py:510
  251.9 17.1 %shard_map.200 = (bf16[1024,768]{1,0:T(8,128)(2,1)}, f32[1024,768]{1,0:T(8,128)}, bf16[1024,768]{1,0:T(8,128)(2,1)}, bf16[1024,768]{1,0:T(8,128)(2,1)}, f32[1024...) custom-call(f32[1280,768]{1,0:T(8,128)} %get-tuple-element.37.out_ref, f32[1280,768]{1,0:T(8,128)} %get-tuple-element.38.back_ref, ...), custom_call_target="tpu_custom_call" | custom-call | tf_op jit(solution)/shard_map/pallas_call | solution.py:571
  269.1 38.0 %shard_map.201 = (bf16[1024,768]{1,0:T(8,128)(2,1)}, bf16[1024,768]{1,0:T(8,128)(2,1)}, bf16[1024,768]{1,0:T(8,128)(2,1)}) custom-call(s32[1]{0:T(128)S(6)} %copy.45.len_ref, bf16[1024,2304]{1,0:T(8,128)(2,1)} %get-tuple-element.33.q_ref.k_ref.v_ref, bf16[1024,2304]{1,0:T(8,128)(2,1)} %get-tuple-element.33.q_ref.k_ref.v_ref, ...), custom_call_target="tpu_custom_call" | custom-call | tf_op jit(solution)/shard_map/pallas_call | solution.py:678
  307.1 16.4 %shard_map.202 = (bf16[1024,768]{1,0:T(8,128)(2,1)}, bf16[768,3200]{1,0:T(8,128)(2,1)}) custom-call(bf16[1024,768]{1,0:T(8,128)(2,1)} %get-tuple-element.44.dq_ref, bf16[1024,768]{1,0:T(8,128)(2,1)} %get-tuple-element.45.dk_ref, bf16[1024,768]{1,0:T(8,128)(2,1)} %get-tuple-element.46.dv_ref, bf16[1024,768]{1,0:T(8,128)(2,1)} %get-tuple-element.47.normed_ref, ...), custom_call_target="tpu_custom_call" | custom-call | tf_op jit(solution)/shard_map/pallas_call | solution.py:743
  323.5 29.6 %shard_map.203 = f32[1,24,3200]{2,1,0:T(8,128)} custom-call(bf16[32,1,24,3200]{3,2,1,0:T(8,128)(2,1)} %bitcast.34), custom_call_target="tpu_custom_call" | custom-call | tf_op jit(solution)/shard_map/pallas_call | solution.py:286
  353.2 1.6 slice_reduce_fusion
  354.8 1.5 slice.61
  356.3 1.6 slice.60
  357.9 106.3 %shard_map.204 = f32[4,96,768]{2,1,0:T(8,128)} custom-call(bf16[32,4,96,768]{3,2,1,0:T(8,128)(2,1)} %bitcast.33), custom_call_target="tpu_custom_call" | custom-call | tf_op jit(solution)/shard_map/pallas_call | solution.py:286
  464.2 1.3 slice_bitcast_fusion
  465.6 1.3 copy.42
  466.8 1.3 copy.41
  (2 shorter events, 0.1 us)
Async XLA Ops:
  0.6 10.2 %copy-start = (bf16[1024,768]{1,0:T(8,128)(2,1)S(1)}, bf16[1024,768]{1,0:T(8,128)(2,1)}, u32[]{:S(2)}) copy-start(bf16[1024,768]{1,0:T(8,128)(2,1)} %grad_ref.1) | copy-start | bytes 4718596
